TPU v7x, 512 devices: a whole 4x4x16 slice. The times are simulated.
512 devices in a mesh: section: 16 (over x, z_hi), seq: 16 (over z_lo, y), mp: 2 (over core).
Axes of the slice: x: 4, y: 4, z: 16 (z_hi: 4, z_lo: 4; z = z_hi * 4 + z_lo), core: 2. Of those that a mesh axis runs over, the one named last changes fastest.
Arguments:
- query_rows: bfloat16 [16, 2048, 2048], P('section', 'seq', 'mp'), may hold values from -150 to 150
- key_row_matrix: bfloat16 [16, 2048, 1024], P('section', 'seq', 'mp'), may hold values from -13 to 13
- value_row_matrix: bfloat16 [16, 2048, 1024], P('section', 'seq', 'mp'), may hold values from -6 to 6
- out_grad: bfloat16 [16, 2048, 2048], P('section', 'seq', 'mp'), may hold values from -24 to 24
- w_query: bfloat16 [16, 5376, 2048], P('section', 'seq', 'mp'), may hold values from -0.078125 to 0.078125
- key_weight: bfloat16 [16, 5376, 1024], P('section', 'seq', 'mp'), may hold values from -0.078125 to 0.078125
- value_weight: bfloat16 [16, 5376, 1024], P('section', 'seq', 'mp'), may hold values from -0.078125 to 0.078125
- doc_ids: int32 [16, 2048], P('section'), may hold values from 0 to 5, never falling along the last dimension, each value on 1 to 682 neighbouring positions
Outputs:
- upstream: bfloat16 [16, 2048, 5376], P('section', None, ('seq', 'mp'))
All inputs are finite; a program needn't handle non-finite values.
Results may differ from a plain program's by a relative error of at most 0.0071.
Values may be sent and summed in bfloat16 or wider, within the bound.
A program may use at most 64 MiB of HBM per device.

v0:
```python
from functools import reduce
import math
import jax
import jax.numpy as jnp
from jax import lax
from jax.sharding import PartitionSpec as P

HEAD_WIDTH = 128
WINDOW = 512


def from_behind(shard, axis, by):
    size = lax.axis_size(axis)
    pairs = [(i, i + by) for i in range(size) if 0 <= i + by < size]
    return lax.ppermute(shard, axis, pairs)


def passed_along(block, axis, distance):
    devices = range(lax.axis_size(axis))
    route = [((i - distance) % len(devices), i) for i in devices]
    return lax.ppermute(block, axis, route)


def per_device(
    query_rows,
    key_row_matrix,
    value_row_matrix,
    out_grad,
    w_query,
    key_weight,
    value_weight,
    doc_ids,
):
    query_here = query_rows[0]
    key_here = key_row_matrix[0]
    value_here = value_row_matrix[0]
    grad_here = out_grad[0]
    documents = doc_ids[0]
    row_count = query_here.shape[0]
    kv_cols = key_here.shape[1]
    kv_heads = kv_cols // HEAD_WIDTH
    group_width = query_here.shape[1] // kv_cols
    scaling = 1.0 / math.sqrt(HEAD_WIDTH)
    seq_count = lax.axis_size("seq")
    seq_place = lax.axis_index("seq")
    reach_now = min((WINDOW - 1) // row_count + 1, seq_count - 1)
    kv_local = jnp.concatenate([key_here, value_here], axis=1)
    rim_blocks = [from_behind(kv_local, "seq", distance) for distance in range(reach_now, 0, -1)]
    kv_blocks = rim_blocks + [kv_local]
    block_total = len(kv_blocks)
    span_rows = block_total * row_count
    first_row = seq_place * row_count
    padded_docs = jnp.concatenate([jnp.full((reach_now * row_count,), -1, jnp.int32), documents])
    key_docs = lax.dynamic_slice_in_dim(padded_docs, first_row, span_rows, 0)
    query_docs = lax.dynamic_slice_in_dim(documents, first_row, row_count, 0)
    query_pos = first_row + jnp.arange(row_count, dtype=jnp.int32)
    key_pos = first_row - reach_now * row_count + jnp.arange(span_rows, dtype=jnp.int32)
    offset = query_pos[:, None] - key_pos[None, :]
    allowed = (query_docs[:, None] == key_docs[None, :]) & (offset >= 0) & (offset < WINDOW)
    query_split = query_here.reshape(row_count, kv_heads, group_width, HEAD_WIDTH)
    grad_split = grad_here.reshape(row_count, kv_heads, group_width, HEAD_WIDTH)
    block_masks = [
        allowed[:, block_index * row_count : (block_index + 1) * row_count]
        for block_index in range(block_total)
    ]
    block_keys = [
        kv_block[:, :kv_cols].reshape(row_count, kv_heads, HEAD_WIDTH) for kv_block in kv_blocks
    ]
    block_values = [
        kv_block[:, kv_cols:].reshape(row_count, kv_heads, HEAD_WIDTH) for kv_block in kv_blocks
    ]

    def score_pair(key_block, mask_now):

        def make_fn():
            product = (
                jnp.einsum(
                    "igrd,jgd->grij", query_split, key_block, preferred_element_type=jnp.float32
                )
                * scaling
            )
            return jnp.where(mask_now[None, None], product, -jnp.inf)

        def empty_fn():
            return jnp.full((kv_heads, group_width, row_count, row_count), -jnp.inf, jnp.float32)

        return (make_fn, empty_fn)

    scores = []
    for block_index in range(block_total):
        make_fn, empty_fn = score_pair(block_keys[block_index], block_masks[block_index])
        scores.append(make_fn())
    row_max = reduce(
        jnp.maximum, [jnp.max(score_now, axis=-1, keepdims=True) for score_now in scores]
    )
    raised = [jnp.exp(score_now - row_max) for score_now in scores]
    row_total = reduce(
        jnp.add, [jnp.sum(raised_now, axis=-1, keepdims=True) for raised_now in raised]
    )
    weights_full = [raised_now / row_total for raised_now in raised]
    weights_half = [weight_now.astype(jnp.bfloat16) for weight_now in weights_full]

    def value_pair(weight_half, value_block):

        def make_fn():
            return jnp.einsum(
                "grij,jgd->igrd", weight_half, value_block, preferred_element_type=jnp.float32
            )

        def empty_fn():
            return jnp.zeros((row_count, kv_heads, group_width, HEAD_WIDTH), jnp.float32)

        return (make_fn, empty_fn)

    attended_terms = []
    for block_index in range(block_total):
        make_fn, empty_fn = value_pair(weights_half[block_index], block_values[block_index])
        attended_terms.append(make_fn())
    attended = reduce(jnp.add, attended_terms)
    delta_row = jnp.transpose(
        jnp.sum(grad_split.astype(jnp.float32) * attended, axis=-1), (1, 2, 0)
    )

    def grad_pair(weight_full, weight_half, key_block, value_block):

        def make_fn():
            grad_weights = jnp.einsum(
                "igrd,jgd->grij", grad_split, value_block, preferred_element_type=jnp.float32
            )
            grad_scores = (weight_full * (grad_weights - delta_row[..., None])).astype(jnp.bfloat16)
            query_term = jnp.einsum(
                "grij,jgd->igrd", grad_scores, key_block, preferred_element_type=jnp.float32
            )
            key_term = (
                jnp.einsum(
                    "grij,igrd->jgd", grad_scores, query_split, preferred_element_type=jnp.float32
                )
                * scaling
            )
            value_term = jnp.einsum(
                "grij,igrd->jgd", weight_half, grad_split, preferred_element_type=jnp.float32
            )
            kv_term = jnp.concatenate(
                [key_term.reshape(row_count, kv_cols), value_term.reshape(row_count, kv_cols)],
                axis=1,
            )
            return (query_term, kv_term)

        def empty_fn():
            return (
                jnp.zeros((row_count, kv_heads, group_width, HEAD_WIDTH), jnp.float32),
                jnp.zeros((row_count, 2 * kv_cols), jnp.float32),
            )

        return (make_fn, empty_fn)

    query_terms = []
    kv_terms = []
    for block_index in range(block_total):
        make_fn, empty_fn = grad_pair(
            weights_full[block_index],
            weights_half[block_index],
            block_keys[block_index],
            block_values[block_index],
        )
        query_term, kv_term = make_fn()
        query_terms.append(query_term)
        kv_terms.append(kv_term)
    query_grad = (
        (reduce(jnp.add, query_terms) * scaling)
        .astype(jnp.bfloat16)
        .reshape(row_count, kv_heads * group_width * HEAD_WIDTH)
    )
    kv_total = kv_terms[-1]
    for distance in range(1, reach_now + 1):
        kv_total = kv_total + from_behind(kv_terms[reach_now - distance], "seq", -distance)
    grad_matrix = jnp.concatenate([query_grad, kv_total.astype(jnp.bfloat16)], axis=1)
    weights_all = jnp.concatenate([w_query[0], key_weight[0], value_weight[0]], axis=1)
    partial_grad = lax.dot_general(
        lax.all_gather(grad_matrix, "seq", axis=0, tiled=True),
        weights_all,
        (((1,), (1,)), ((), ())),
        preferred_element_type=jnp.float32,
    )
    summed = lax.psum_scatter(partial_grad, "mp", scatter_dimension=1, tiled=True)
    grad_input = summed.astype(jnp.bfloat16)
    upstream = passed_along(grad_input, "section", -1)
    return upstream[None]


def solution(mesh):
    placed = (
        P("section", "seq", "mp"),
        P("section", "seq", "mp"),
        P("section", "seq", "mp"),
        P("section", "seq", "mp"),
        P("section", "seq", "mp"),
        P("section", "seq", "mp"),
        P("section", "seq", "mp"),
        P("section", None),
    )
    return jax.shard_map(
        per_device,
        mesh=mesh,
        in_specs=placed,
        out_specs=P("section", None, ("seq", "mp")),
        check_vma=False,
    )
```

profile of v0, /device:TPU:8, one launch (start us, length us, event | category | flops | bytes accessed | tf_op | source)
XLA Modules:
  0.0 336.0 jit_solution(13602698483485576235)
XLA Ops:
  6.5 1.1 copy.60
  7.6 1.0 copy.61
  8.7 3.5 %collective-permute-start.3 = (bf16[128,1024]{0,1:T(8,128)(2,1)S(1)}, bf16[128,1024]{0,1:T(8,128)(2,1)S(1)}, u32[]{:S(2)}, u32[]{:S(2)}) collective-permute-start(bf16[128,1024]{0,1:T(8,128)(2,1)S(1)} %pad_maximum_fusion.5), channel_id=1, source_target_pairs={{0,2},{2,4},{4,6},{6,8},{8,10},{10,12},{12,14},{14,16},{16,18},{18... | collective-permute-start | bytes 786440 | tf_op jit(solution)/shard_map/ppermute | solution.py:15
  12.2 4.2 %collective-permute-start.2 = (bf16[128,1024]{0,1:T(8,128)(2,1)S(1)}, bf16[128,1024]{0,1:T(8,128)(2,1)S(1)}, u32[]{:S(2)}, u32[]{:S(2)}) collective-permute-start(bf16[128,1024]{0,1:T(8,128)(2,1)S(1)} %pad_maximum_fusion.5), channel_id=1, source_target_pairs={{0,4},{2,6},{4,8},{6,10},{8,12},{10,14},{12,16},{14,18},{16,20},{1... | collective-permute-start | bytes 786440 | tf_op jit(solution)/shard_map/ppermute | solution.py:15
  16.4 4.3 %collective-permute-start.1 = (bf16[128,1024]{0,1:T(8,128)(2,1)S(1)}, bf16[128,1024]{0,1:T(8,128)(2,1)S(1)}, u32[]{:S(2)}, u32[]{:S(2)}) collective-permute-start(bf16[128,1024]{0,1:T(8,128)(2,1)S(1)} %pad_maximum_fusion.5), channel_id=1, source_target_pairs={{0,6},{2,8},{4,10},{6,12},{8,14},{10,16},{12,18},{14,20},{16,22},{... | collective-permute-start | bytes 786440 | tf_op jit(solution)/shard_map/ppermute | solution.py:15
  20.7 3.8 %collective-permute-start = (bf16[128,1024]{0,1:T(8,128)(2,1)S(1)}, bf16[128,1024]{0,1:T(8,128)(2,1)S(1)}, u32[]{:S(2)}, u32[]{:S(2)}) collective-permute-start(bf16[128,1024]{0,1:T(8,128)(2,1)S(1)} %pad_maximum_fusion.5), channel_id=1, source_target_pairs={{0,8},{2,10},{4,12},{6,14},{8,16},{10,18},{12,20},{14,22},{16,24},... | collective-permute-start | bytes 786440 | tf_op jit(solution)/shard_map/ppermute | solution.py:15
  26.3 0.9 reshape_squeeze.13
  27.2 0.9 reshape_squeeze.15
  28.3 1.1 copy.189
  29.9 1.5 collective-permute-done
  39.3 1.3 collective-permute-start.5
  40.6 1.3 collective-permute-start.6
  41.9 1.9 collective-permute-start.4
  43.9 1.3 collective-permute-start.7
  45.8 13.9 %collective-permute-done.5 = f32[128,1024]{0,1:T(8,128)S(1)} collective-permute-done((f32[128,1024]{0,1:T(8,128)S(1)}, f32[128,1024]{0,1:T(8,128)S(1)}, u32[]{:S(2)}, u32[]{:S(2)}) %collective-permute-start.5) | collective-permute-done | bytes 524320 | tf_op jit(solution)/shard_map/ppermute | solution.py:15
  59.7 14.0 %collective-permute-done.6 = f32[128,1024]{0,1:T(8,128)S(1)} collective-permute-done((f32[128,1024]{0,1:T(8,128)S(1)}, f32[128,1024]{0,1:T(8,128)S(1)}, u32[]{:S(2)}, u32[]{:S(2)}) %collective-permute-start.6) | collective-permute-done | bytes 524320 | tf_op jit(solution)/shard_map/ppermute | solution.py:15
  73.6 8.8 %collective-permute-done.7 = f32[128,1024]{0,1:T(8,128)S(1)} collective-permute-done((f32[128,1024]{0,1:T(8,128)S(1)}, f32[128,1024]{0,1:T(8,128)S(1)}, u32[]{:S(2)}, u32[]{:S(2)}) %collective-permute-start.7) | collective-permute-done | bytes 524320 | tf_op jit(solution)/shard_map/ppermute | solution.py:15
  83.5 145.0 %all-gather.2.cloned.1.call-done = bf16[2048,2048]{0,1:T(8,128)(2,1)} async-done(((bf16[128,2048]{0,1:T(8,128)(2,1)}), bf16[2048,2048]{0,1:T(8,128)(2,1)}) %all-gather.2.cloned.1.call-update) | async-done | bytes 8388624 | tf_op jit(solution)/shard_map/all_gather | solution.py:180
  228.5 8.0 %fusion = f32[2048,336]{0,1:T(8,128)} fusion(bf16[2048,2048]{0,1:T(8,128)(2,1)} %all-gather.2.cloned.1.call-done, bf16[336,512]{1,0:T(8,128)(2,1)S(1)} %bitcast.386, bf16[336,512]{1,0:T(8,128)(2,1)S(1)} %bitcast.387, bf16[336,1024]{1,0:T(8,128)(2,1)S(1)} %bitcast.385), kind=kOutput, calls=%fused_computation | convolution fusion | flops 2822701056 | bytes 12517376 | tf_op jit(solution)/shard_map/dot_general | solution.py:179
  236.5 20.4 %reduce-scatter.2.cloned.1.call-done = f32[2048,168]{0,1:T(8,128)} async-done(((f32[2048,336]{0,1:T(8,128)}), f32[2048,168]{0,1:T(8,128)}) %reduce-scatter.2.cloned.1.call-update) | async-done | bytes 1376272 | tf_op jit(solution)/shard_map/reduce_scatter | solution.py:185
  257.0 1.4 convert_element_type.55
  258.4 10.5 %collective-permute-start.8 = (bf16[2048,168]{0,1:T(8,128)(2,1)S(1)}, bf16[2048,168]{0,1:T(8,128)(2,1)S(1)}, u32[]{:S(2)}, u32[]{:S(2)}) collective-permute-start(bf16[2048,168]{0,1:T(8,128)(2,1)S(1)} %convert_element_type.55), channel_id=1, source_target_pairs={{32,0},{64,32},{96,64},{128,96},{160,128},{192,160},{224,192},{256... | collective-permute-start | bytes 2064392 | tf_op jit(solution)/shard_map/ppermute | solution.py:21
  268.9 59.4 %collective-permute-done.8 = bf16[2048,168]{0,1:T(8,128)(2,1)S(1)} collective-permute-done((bf16[2048,168]{0,1:T(8,128)(2,1)S(1)}, bf16[2048,168]{0,1:T(8,128)(2,1)S(1)}, u32[]{:S(2)}, u32[]{:S(2)}) %collective-permute-start.8) | collective-permute-done | bytes 688160 | tf_op jit(solution)/shard_map/ppermute | solution.py:21
  328.3 0.8 copy.195
  (68 shorter events, 11.6 us)
Async XLA Ops:
  6.5 22.9 %copy-start = (bf16[1,128,1024]{2,1,0:T(8,128)(2,1)S(1)}, bf16[1,128,1024]{2,1,0:T(8,128)(2,1)}, u32[]{:S(2)}) copy-start(bf16[1,128,1024]{2,1,0:T(8,128)(2,1)} %param.11) | copy-start | bytes 786436
  6.5 222.0 %all-gather.2.cloned.1.call-start = ((), (), s32[]{:S(2)}) async-start(), calls=%async_computation.1 | async-start | bytes 8912896 | tf_op jit(solution)/shard_map/all_gather | solution.py:180
  8.7 23.7 %collective-permute-start.3 = (bf16[128,1024]{0,1:T(8,128)(2,1)S(1)}, bf16[128,1024]{0,1:T(8,128)(2,1)S(1)}, u32[]{:S(2)}, u32[]{:S(2)}) collective-permute-start(bf16[128,1024]{0,1:T(8,128)(2,1)S(1)} %pad_maximum_fusion.5), channel_id=1, source_target_pairs={{0,2},{2,4},{4,6},{6,8},{8,10},{10,12},{12,14},{14,16},{16,18},{18... | collective-permute-start | bytes 786440 | tf_op jit(solution)/shard_map/ppermute | solution.py:15
  12.2 19.8 %collective-permute-start.2 = (bf16[128,1024]{0,1:T(8,128)(2,1)S(1)}, bf16[128,1024]{0,1:T(8,128)(2,1)S(1)}, u32[]{:S(2)}, u32[]{:S(2)}) collective-permute-start(bf16[128,1024]{0,1:T(8,128)(2,1)S(1)} %pad_maximum_fusion.5), channel_id=1, source_target_pairs={{0,4},{2,6},{4,8},{6,10},{8,12},{10,14},{12,16},{14,18},{16,20},{1... | collective-permute-start | bytes 786440 | tf_op jit(solution)/shard_map/ppermute | solution.py:15
  16.4 15.3 %collective-permute-start.1 = (bf16[128,1024]{0,1:T(8,128)(2,1)S(1)}, bf16[128,1024]{0,1:T(8,128)(2,1)S(1)}, u32[]{:S(2)}, u32[]{:S(2)}) collective-permute-start(bf16[128,1024]{0,1:T(8,128)(2,1)S(1)} %pad_maximum_fusion.5), channel_id=1, source_target_pairs={{0,6},{2,8},{4,10},{6,12},{8,14},{10,16},{12,18},{14,20},{16,22},{... | collective-permute-start | bytes 786440 | tf_op jit(solution)/shard_map/ppermute | solution.py:15
  20.7 10.6 %collective-permute-start = (bf16[128,1024]{0,1:T(8,128)(2,1)S(1)}, bf16[128,1024]{0,1:T(8,128)(2,1)S(1)}, u32[]{:S(2)}, u32[]{:S(2)}) collective-permute-start(bf16[128,1024]{0,1:T(8,128)(2,1)S(1)} %pad_maximum_fusion.5), channel_id=1, source_target_pairs={{0,8},{2,10},{4,12},{6,14},{8,16},{10,18},{12,20},{14,22},{16,24},... | collective-permute-start | bytes 786440 | tf_op jit(solution)/shard_map/ppermute | solution.py:15
  39.3 20.4 %collective-permute-start.5 = (f32[128,1024]{0,1:T(8,128)S(1)}, f32[128,1024]{0,1:T(8,128)S(1)}, u32[]{:S(2)}, u32[]{:S(2)}) collective-permute-start(f32[128,1024]{0,1:T(8,128)S(1)} %pad_maximum_fusion.1), channel_id=1, source_target_pairs={{4,0},{6,2},{8,4},{10,6},{12,8},{14,10},{16,12},{18,14},{20,16},{2... | collective-permute-start | bytes 1572872 | tf_op jit(solution)/shard_map/ppermute | solution.py:15
  40.6 33.0 %collective-permute-start.6 = (f32[128,1024]{0,1:T(8,128)S(1)}, f32[128,1024]{0,1:T(8,128)S(1)}, u32[]{:S(2)}, u32[]{:S(2)}) collective-permute-start(f32[128,1024]{0,1:T(8,128)S(1)} %pad_maximum_fusion.2), channel_id=1, source_target_pairs={{6,0},{8,2},{10,4},{12,6},{14,8},{16,10},{18,12},{20,14},{22,16},{... | collective-permute-start | bytes 1572872 | tf_op jit(solution)/shard_map/ppermute | solution.py:15
  41.9 31.7 %collective-permute-start.4 = (f32[128,1024]{0,1:T(8,128)S(1)}, f32[128,1024]{0,1:T(8,128)S(1)}, u32[]{:S(2)}, u32[]{:S(2)}) collective-permute-start(f32[128,1024]{0,1:T(8,128)S(1)} %pad_maximum_fusion), channel_id=1, source_target_pairs={{2,0},{4,2},{6,4},{8,6},{10,8},{12,10},{14,12},{16,14},{18,16},{20... | collective-permute-start | bytes 1572872 | tf_op jit(solution)/shard_map/ppermute | solution.py:15
  43.9 38.6 %collective-permute-start.7 = (f32[128,1024]{0,1:T(8,128)S(1)}, f32[128,1024]{0,1:T(8,128)S(1)}, u32[]{:S(2)}, u32[]{:S(2)}) collective-permute-start(f32[128,1024]{0,1:T(8,128)S(1)} %pad_maximum_fusion.3), channel_id=1, source_target_pairs={{8,0},{10,2},{12,4},{14,6},{16,8},{18,10},{20,12},{22,14},{24,16},... | collective-permute-start | bytes 1572872 | tf_op jit(solution)/shard_map/ppermute | solution.py:15
  45.7 182.8 %copy-start.1 = (bf16[1,336,1024]{2,1,0:T(8,128)(2,1)S(1)}, bf16[1,336,1024]{2,1,0:T(8,128)(2,1)}, u32[]{:S(2)}) copy-start(bf16[1,336,1024]{2,1,0:T(8,128)(2,1)} %param.12) | copy-start | bytes 2064388
  45.7 182.8 %copy-start.2 = (bf16[1,336,512]{2,1,0:T(8,128)(2,1)S(1)}, bf16[1,336,512]{2,1,0:T(8,128)(2,1)}, u32[]{:S(2)}) copy-start(bf16[1,336,512]{2,1,0:T(8,128)(2,1)} %param.14) | copy-start | bytes 1032196
  45.8 182.7 %copy-start.3 = (bf16[1,336,512]{2,1,0:T(8,128)(2,1)S(1)}, bf16[1,336,512]{2,1,0:T(8,128)(2,1)}, u32[]{:S(2)}) copy-start(bf16[1,336,512]{2,1,0:T(8,128)(2,1)} %param.13) | copy-start | bytes 1032196
  83.5 173.5 %reduce-scatter.2.cloned.1.call-start = ((), (), s32[]{:S(2)}) async-start(), calls=%async_computation.2 | async-start | bytes 4128768 | tf_op jit(solution)/shard_map/reduce_scatter | solution.py:185
  258.4 69.9 %collective-permute-start.8 = (bf16[2048,168]{0,1:T(8,128)(2,1)S(1)}, bf16[2048,168]{0,1:T(8,128)(2,1)S(1)}, u32[]{:S(2)}, u32[]{:S(2)}) collective-permute-start(bf16[2048,168]{0,1:T(8,128)(2,1)S(1)} %convert_element_type.55), channel_id=1, source_target_pairs={{32,0},{64,32},{96,64},{128,96},{160,128},{192,160},{224,192},{256... | collective-permute-start | bytes 2064392 | tf_op jit(solution)/shard_map/ppermute | solution.py:21
Sparse Core Ops, SparseCore 0:
  83.6 144.8 all-gather.1
  236.7 20.2 reduce-scatter.1
where the time goes:
time: 337 us; the launch traced here: 336 us
  waiting for transfers between devices  263 us (78%)
  starting transfers between devices  32.2 us (10%)
  matrix products  15.4 us (5%)
  between operations  13.9 us (4%)
  local copies, waits for them, and re-layouts  7.01 us (2%)
  other arithmetic  4.5 us (1%)
    all_gather x1, waiting for transfers between devices, per_device(): lax.all_gather(grad_matrix, 'seq', axis=0, tiled=True)  145 us
    ppermute x1, waiting for transfers between devices, passed_along(): return lax.ppermute(block, axis, route)  59.4 us
    ppermute x8, waiting for transfers between devices, from_behind(): return lax.ppermute(shard, axis, pairs)  38.2 us
    ppermute x8, starting transfers between devices, from_behind(): return lax.ppermute(shard, axis, pairs)  21.6 us
    reduce_scatter x1, waiting for transfers between devices, per_device(): lax.psum_scatter(partial_grad, 'mp', scatter_dimension=1, tiled=True)  20.4 us
    ppermute x1, starting transfers between devices, passed_along(): return lax.ppermute(block, axis, route)  10.5 us
    dot_general x1, matrix products, per_device(): lax.dot_general(lax.all_gather(grad_matrix, 'seq', axis=0, tiled=True), w...  8.02 us
  transfers between devices with their start and end apart: 11, of which 7 were waited for; matrix products, arithmetic and copies ran while one was open for 2% of the time, Pallas kernels for 0%

commit v1 on v0

--- a/solution.py
+++ b/solution.py
@@ -177,7 +177,9 @@
     grad_matrix = jnp.concatenate([query_grad, kv_total.astype(jnp.bfloat16)], axis=1)
     weights_all = jnp.concatenate([w_query[0], key_weight[0], value_weight[0]], axis=1)
     partial_grad = lax.dot_general(
-        lax.all_gather(grad_matrix, "seq", axis=0, tiled=True),
+        jnp.concatenate(
+            lax.all_to_all(jnp.stack([grad_matrix] * lax.axis_size("seq")), "seq", 0, 0), axis=0
+        ),
         weights_all,
         (((1,), (1,)), ((), ())),
         preferred_element_type=jnp.float32,

time: 337 us -> 389 us (1.15)
  blocking collectives: 0 us -> 197 us
  waiting for transfers between devices: 263 us -> 121 us
    all_to_all x0 -> x1, blocking collectives: none -> 197 us  [per_device(): lax.all_to_all(jnp.stack([grad_matrix] * lax.axis_size('seq')), 'seq', 0, 0)]
    all_gather x1 -> x0, waiting for transfers between devices: 145 us -> none  [per_device(): lax.all_gather(grad_matrix, 'seq', axis=0, tiled=True)]
  transfers between devices with their start and end apart: 11 -> 10, of which waited for: 7 -> 6; matrix products, arithmetic and copies ran while one was open for 2% -> 2% of each run, Pallas kernels for 0% -> 0%
where the time goes in v1:
time: 389 us; the launch traced here: 388 us
  blocking collectives  197 us (51%)
  waiting for transfers between devices  121 us (31%)
  starting transfers between devices  32.2 us (8%)
  between operations  13.9 us (4%)
  matrix products  12 us (3%)
  local copies, waits for them, and re-layouts  8.28 us (2%)
    all_to_all x1, blocking collectives, per_device(): lax.all_to_all(jnp.stack([grad_matrix] * lax.axis_size('seq')), 'seq', 0, 0)  197 us
    ppermute x1, waiting for transfers between devices, passed_along(): return lax.ppermute(block, axis, route)  59.4 us
    ppermute x8, waiting for transfers between devices, from_behind(): return lax.ppermute(shard, axis, pairs)  38.2 us
    reduce_scatter x1, waiting for transfers between devices, per_device(): lax.psum_scatter(partial_grad, 'mp', scatter_dimension=1, tiled=True)  23.5 us
    ppermute x8, starting transfers between devices, from_behind(): return lax.ppermute(shard, axis, pairs)  21.6 us
    ppermute x1, starting transfers between devices, passed_along(): return lax.ppermute(block, axis, route)  10.5 us
  transfers between devices with their start and end apart: 10, of which 6 were waited for; matrix products, arithmetic and copies ran while one was open for 2% of the time, Pallas kernels for 0%

profile of v1, /device:TPU:8, one launch (start us, length us, event | category | flops | bytes accessed | tf_op | source)
XLA Modules:
  0.0 388.4 jit_solution(7268377879816939848)
XLA Ops:
  6.5 1.1 copy.61
  7.6 1.0 copy.62
  8.7 3.5 collective-permute-start.3
  12.2 4.2 %collective-permute-start.2 = (bf16[128,1024]{0,1:T(8,128)(2,1)S(1)}, bf16[128,1024]{0,1:T(8,128)(2,1)S(1)}, u32[]{:S(2)}, u32[]{:S(2)}) collective-permute-start(bf16[128,1024]{0,1:T(8,128)(2,1)S(1)} %pad_maximum_fusion.5), channel_id=1, source_target_pairs={{0,4},{2,6},{4,8},{6,10},{8,12},{10,14},{12,16},{14,18},{16,20},{1... | collective-permute-start | bytes 786440 | tf_op jit(solution)/shard_map/ppermute | solution.py:15
  16.4 4.3 %collective-permute-start.1 = (bf16[128,1024]{0,1:T(8,128)(2,1)S(1)}, bf16[128,1024]{0,1:T(8,128)(2,1)S(1)}, u32[]{:S(2)}, u32[]{:S(2)}) collective-permute-start(bf16[128,1024]{0,1:T(8,128)(2,1)S(1)} %pad_maximum_fusion.5), channel_id=1, source_target_pairs={{0,6},{2,8},{4,10},{6,12},{8,14},{10,16},{12,18},{14,20},{16,22},{... | collective-permute-start | bytes 786440 | tf_op jit(solution)/shard_map/ppermute | solution.py:15
  20.7 3.8 collective-permute-start
  26.3 0.9 reshape_squeeze.13
  27.2 0.9 reshape_squeeze.15
  28.3 1.1 copy.191
  29.9 1.5 collective-permute-done
  39.3 1.3 collective-permute-start.5
  40.6 1.3 collective-permute-start.6
  42.0 1.9 collective-permute-start.4
  44.0 1.3 collective-permute-start.7
  45.8 13.9 %collective-permute-done.5 = f32[128,1024]{0,1:T(8,128)S(1)} collective-permute-done((f32[128,1024]{0,1:T(8,128)S(1)}, f32[128,1024]{0,1:T(8,128)S(1)}, u32[]{:S(2)}, u32[]{:S(2)}) %collective-permute-start.5) | collective-permute-done | bytes 524320 | tf_op jit(solution)/shard_map/ppermute | solution.py:15
  59.7 14.0 %collective-permute-done.6 = f32[128,1024]{0,1:T(8,128)S(1)} collective-permute-done((f32[128,1024]{0,1:T(8,128)S(1)}, f32[128,1024]{0,1:T(8,128)S(1)}, u32[]{:S(2)}, u32[]{:S(2)}) %collective-permute-start.6) | collective-permute-done | bytes 524320 | tf_op jit(solution)/shard_map/ppermute | solution.py:15
  73.7 8.8 %collective-permute-done.7 = f32[128,1024]{0,1:T(8,128)S(1)} collective-permute-done((f32[128,1024]{0,1:T(8,128)S(1)}, f32[128,1024]{0,1:T(8,128)S(1)}, u32[]{:S(2)}, u32[]{:S(2)}) %collective-permute-start.7) | collective-permute-done | bytes 524320 | tf_op jit(solution)/shard_map/ppermute | solution.py:15
  82.9 1.1 stack.2
  84.0 197.2 %all_to_all.5 = bf16[16,128,2048]{2,1,0:T(8,128)(2,1)S(1)} all-to-all(bf16[16,128,2048]{2,1,0:T(8,128)(2,1)S(1)} %stack.2), channel_id=1, replica_groups=mesh['section'=16,'seq'=16,'mp'=2] {'seq'}, dimensions={0} | all-to-all | bytes 16777216 | tf_op jit(solution)/shard_map/all_to_all | solution.py:181
  281.2 4.6 %fusion = f32[2048,336]{0,1:T(8,128)} fusion(bf16[2048,2048]{1,0:T(8,128)(2,1)S(1)} %bitcast.324, bf16[336,512]{1,0:T(8,128)(2,1)S(1)} %bitcast.388, bf16[336,512]{1,0:T(8,128)(2,1)S(1)} %bitcast.389, bf16[336,1024]{1,0:T(8,128)(2,1)S(1)} %bitcast.387), kind=kOutput, calls=%fused_computation | convolution fusion | flops 2822701056 | bytes 12517376 | tf_op jit(solution)/shard_map/dot_general | solution.py:179
  285.8 23.5 %reduce-scatter.2.cloned.1.call-done = f32[2048,168]{0,1:T(8,128)} async-done(((f32[2048,336]{0,1:T(8,128)}), f32[2048,168]{0,1:T(8,128)}) %reduce-scatter.2.cloned.1.call-update) | async-done | bytes 1376272 | tf_op jit(solution)/shard_map/reduce_scatter | solution.py:187
  309.4 1.4 convert_element_type.55
  310.8 10.5 %collective-permute-start.8 = (bf16[2048,168]{0,1:T(8,128)(2,1)S(1)}, bf16[2048,168]{0,1:T(8,128)(2,1)S(1)}, u32[]{:S(2)}, u32[]{:S(2)}) collective-permute-start(bf16[2048,168]{0,1:T(8,128)(2,1)S(1)} %convert_element_type.55), channel_id=1, source_target_pairs={{32,0},{64,32},{96,64},{128,96},{160,128},{192,160},{224,192},{256... | collective-permute-start | bytes 2064392 | tf_op jit(solution)/shard_map/ppermute | solution.py:21
  321.3 59.4 %collective-permute-done.8 = bf16[2048,168]{0,1:T(8,128)(2,1)S(1)} collective-permute-done((bf16[2048,168]{0,1:T(8,128)(2,1)S(1)}, bf16[2048,168]{0,1:T(8,128)(2,1)S(1)}, u32[]{:S(2)}, u32[]{:S(2)}) %collective-permute-start.8) | collective-permute-done | bytes 688160 | tf_op jit(solution)/shard_map/ppermute | solution.py:21
  (68 shorter events, 11.9 us)
Async XLA Ops:
  6.5 22.9 %copy-start = (bf16[1,128,1024]{2,1,0:T(8,128)(2,1)S(1)}, bf16[1,128,1024]{2,1,0:T(8,128)(2,1)}, u32[]{:S(2)}) copy-start(bf16[1,128,1024]{2,1,0:T(8,128)(2,1)} %param.11) | copy-start | bytes 786436
  6.5 302.8 %reduce-scatter.2.cloned.1.call-start = ((), (), s32[]{:S(2)}) async-start(), calls=%async_computation.2 | async-start | bytes 4128768 | tf_op jit(solution)/shard_map/reduce_scatter | solution.py:187
  8.7 23.7 %collective-permute-start.3 = (bf16[128,1024]{0,1:T(8,128)(2,1)S(1)}, bf16[128,1024]{0,1:T(8,128)(2,1)S(1)}, u32[]{:S(2)}, u32[]{:S(2)}) collective-permute-start(bf16[128,1024]{0,1:T(8,128)(2,1)S(1)} %pad_maximum_fusion.5), channel_id=1, source_target_pairs={{0,2},{2,4},{4,6},{6,8},{8,10},{10,12},{12,14},{14,16},{16,18},{18... | collective-permute-start | bytes 786440 | tf_op jit(solution)/shard_map/ppermute | solution.py:15
  12.2 19.8 %collective-permute-start.2 = (bf16[128,1024]{0,1:T(8,128)(2,1)S(1)}, bf16[128,1024]{0,1:T(8,128)(2,1)S(1)}, u32[]{:S(2)}, u32[]{:S(2)}) collective-permute-start(bf16[128,1024]{0,1:T(8,128)(2,1)S(1)} %pad_maximum_fusion.5), channel_id=1, source_target_pairs={{0,4},{2,6},{4,8},{6,10},{8,12},{10,14},{12,16},{14,18},{16,20},{1... | collective-permute-start | bytes 786440 | tf_op jit(solution)/shard_map/ppermute | solution.py:15
  16.4 15.3 %collective-permute-start.1 = (bf16[128,1024]{0,1:T(8,128)(2,1)S(1)}, bf16[128,1024]{0,1:T(8,128)(2,1)S(1)}, u32[]{:S(2)}, u32[]{:S(2)}) collective-permute-start(bf16[128,1024]{0,1:T(8,128)(2,1)S(1)} %pad_maximum_fusion.5), channel_id=1, source_target_pairs={{0,6},{2,8},{4,10},{6,12},{8,14},{10,16},{12,18},{14,20},{16,22},{... | collective-permute-start | bytes 786440 | tf_op jit(solution)/shard_map/ppermute | solution.py:15
  20.7 10.6 %collective-permute-start = (bf16[128,1024]{0,1:T(8,128)(2,1)S(1)}, bf16[128,1024]{0,1:T(8,128)(2,1)S(1)}, u32[]{:S(2)}, u32[]{:S(2)}) collective-permute-start(bf16[128,1024]{0,1:T(8,128)(2,1)S(1)} %pad_maximum_fusion.5), channel_id=1, source_target_pairs={{0,8},{2,10},{4,12},{6,14},{8,16},{10,18},{12,20},{14,22},{16,24},... | collective-permute-start | bytes 786440 | tf_op jit(solution)/shard_map/ppermute | solution.py:15
  39.3 20.4 %collective-permute-start.5 = (f32[128,1024]{0,1:T(8,128)S(1)}, f32[128,1024]{0,1:T(8,128)S(1)}, u32[]{:S(2)}, u32[]{:S(2)}) collective-permute-start(f32[128,1024]{0,1:T(8,128)S(1)} %pad_maximum_fusion.1), channel_id=1, source_target_pairs={{4,0},{6,2},{8,4},{10,6},{12,8},{14,10},{16,12},{18,14},{20,16},{2... | collective-permute-start | bytes 1572872 | tf_op jit(solution)/shard_map/ppermute | solution.py:15
  40.6 33.0 %collective-permute-start.6 = (f32[128,1024]{0,1:T(8,128)S(1)}, f32[128,1024]{0,1:T(8,128)S(1)}, u32[]{:S(2)}, u32[]{:S(2)}) collective-permute-start(f32[128,1024]{0,1:T(8,128)S(1)} %pad_maximum_fusion.2), channel_id=1, source_target_pairs={{6,0},{8,2},{10,4},{12,6},{14,8},{16,10},{18,12},{20,14},{22,16},{... | collective-permute-start | bytes 1572872 | tf_op jit(solution)/shard_map/ppermute | solution.py:15
  42.0 31.7 %collective-permute-start.4 = (f32[128,1024]{0,1:T(8,128)S(1)}, f32[128,1024]{0,1:T(8,128)S(1)}, u32[]{:S(2)}, u32[]{:S(2)}) collective-permute-start(f32[128,1024]{0,1:T(8,128)S(1)} %pad_maximum_fusion), channel_id=1, source_target_pairs={{2,0},{4,2},{6,4},{8,6},{10,8},{12,10},{14,12},{16,14},{18,16},{20... | collective-permute-start | bytes 1572872 | tf_op jit(solution)/shard_map/ppermute | solution.py:15
  44.0 38.6 %collective-permute-start.7 = (f32[128,1024]{0,1:T(8,128)S(1)}, f32[128,1024]{0,1:T(8,128)S(1)}, u32[]{:S(2)}, u32[]{:S(2)}) collective-permute-start(f32[128,1024]{0,1:T(8,128)S(1)} %pad_maximum_fusion.3), channel_id=1, source_target_pairs={{8,0},{10,2},{12,4},{14,6},{16,8},{18,10},{20,12},{22,14},{24,16},... | collective-permute-start | bytes 1572872 | tf_op jit(solution)/shard_map/ppermute | solution.py:15
  84.0 197.2 %copy-start.1 = (bf16[1,336,1024]{2,1,0:T(8,128)(2,1)S(1)}, bf16[1,336,1024]{2,1,0:T(8,128)(2,1)}, u32[]{:S(2)}) copy-start(bf16[1,336,1024]{2,1,0:T(8,128)(2,1)} %param.12) | copy-start | bytes 2064388
  84.0 197.2 %copy-start.2 = (bf16[1,336,512]{2,1,0:T(8,128)(2,1)S(1)}, bf16[1,336,512]{2,1,0:T(8,128)(2,1)}, u32[]{:S(2)}) copy-start(bf16[1,336,512]{2,1,0:T(8,128)(2,1)} %param.14) | copy-start | bytes 1032196
  84.0 197.2 %copy-start.3 = (bf16[1,336,512]{2,1,0:T(8,128)(2,1)S(1)}, bf16[1,336,512]{2,1,0:T(8,128)(2,1)}, u32[]{:S(2)}) copy-start(bf16[1,336,512]{2,1,0:T(8,128)(2,1)} %param.13) | copy-start | bytes 1032196
  310.8 69.9 %collective-permute-start.8 = (bf16[2048,168]{0,1:T(8,128)(2,1)S(1)}, bf16[2048,168]{0,1:T(8,128)(2,1)S(1)}, u32[]{:S(2)}, u32[]{:S(2)}) collective-permute-start(bf16[2048,168]{0,1:T(8,128)(2,1)S(1)} %convert_element_type.55), channel_id=1, source_target_pairs={{32,0},{64,32},{96,64},{128,96},{160,128},{192,160},{224,192},{256... | collective-permute-start | bytes 2064392 | tf_op jit(solution)/shard_map/ppermute | solution.py:21
Sparse Core Ops, SparseCore 0:
  286.0 23.3 reduce-scatter.1
